TPU v7x, 256 devices: a whole 4x4x8 slice. The times are simulated.
256 devices in a mesh: view: 8 (over y_lo, x), tile: 32 (over y_hi, z, core).
Axes of the slice: x: 4, y: 4 (y_hi: 2, y_lo: 2; y = y_hi * 2 + y_lo), z: 8, core: 2. Of those that a mesh axis runs over, the one named last changes fastest.
Arguments:
- estimate: float32 [1024, 64, 256], P('tile'), may hold values from 0.5 to 2
- measured: bfloat16 [8, 1024, 64, 256], P('view', 'tile'), may hold values from 0.5 to 2
- blur_profile: float32 [8, 256], P('view'), may hold values from 0.1 to 1
- view_offset: int32 [8], P('view'), may hold values from -6 to 6, as said below
- tile_shift: int32 [8], P('view'), may hold values from 0 to 31
Outputs:
- updated: float32 [1024, 64, 256], P('tile')
Inputs may be any that keep to these rules, and one draw needn't show every extreme that they name: `view_offset`: some view has offset 6 and some other view has offset -6.
All inputs are finite; a program needn't handle non-finite values.
Results may differ from a plain program's by a relative error of at most 0.0016.
Values may be sent and summed in bfloat16 or wider, within the bound.
No kernel may reach another device: no remote copies, remote signals or barrier semaphores. Data moves between devices by JAX's collectives and lax.ppermute only.
A program may use at most 64 MiB of HBM per device.

v0:
```python
import math
import jax
import jax.numpy as jnp
from jax import lax
from jax.sharding import PartitionSpec as P

H = 6
profile_sigma = 48.0


def with_halo(cells, sides, width):
    for axis, dim in sides:
        count = lax.axis_size(axis)
        head = lax.slice_in_dim(cells, 0, width, axis=dim)
        tail = lax.slice_in_dim(cells, cells.shape[dim] - width, cells.shape[dim], axis=dim)
        cells = jnp.concatenate(
            [
                lax.ppermute(tail, axis, [(i, (i + 1) % count) for i in range(count)]),
                cells,
                lax.ppermute(head, axis, [((i + 1) % count, i) for i in range(count)]),
            ],
            axis=dim,
        )
    return cells


def from_behind(block, axis, distance):
    devices = range(lax.axis_size(axis))
    route = [((i - distance) % len(devices), i) for i in devices]
    return lax.ppermute(block, axis, route)


def make_kernel(profile):
    length = profile.shape[0]
    column = jnp.arange(length)
    distance = jnp.minimum(column, length - column).astype(jnp.float32)
    weights = profile * jnp.exp(-distance * distance / (2.0 * profile_sigma * profile_sigma))
    return weights / jnp.sum(weights)


def matmul_high(left, right):
    return jnp.dot(left, right, precision=lax.Precision.HIGHEST, preferred_element_type=jnp.float32)


def body(estimate, measured, blur_profile, view_offset, tile_shift):
    view_count = lax.axis_size("view")
    view_index = lax.axis_index("view")
    blend_weight = (view_index + 1).astype(jnp.float32) / (view_count + 1)
    kernel = make_kernel(blur_profile[0])
    offset = view_offset[0]
    tile_move = tile_shift[0]
    length = estimate.shape[2]
    halo_width = H + 1
    bit_count = (lax.axis_size("tile") - 1).bit_length()
    column = jnp.arange(length)
    phase = column[:, None] * column[None, :] % length
    angle = phase.astype(jnp.float32) * (2.0 * math.pi / length)
    cosine = jnp.cos(angle)
    sine_table = jnp.sin(angle)
    spec_real = matmul_high(kernel, cosine)
    spec_imag = -matmul_high(kernel, sine_table)

    def blur_along(volume, adjoint):
        imag_kernel = -spec_imag if adjoint else spec_imag
        real_part = matmul_high(volume, cosine)
        imag_part = -matmul_high(volume, sine_table)
        out_real = real_part * spec_real - imag_part * imag_kernel
        out_imag = real_part * imag_kernel + imag_part * spec_real
        return (matmul_high(out_real, cosine) - matmul_high(out_imag, sine_table)) / length

    relocated = estimate
    for level in range(bit_count):
        stride = 1 << level
        arrived = from_behind(relocated.astype(jnp.bfloat16), "tile", -stride).astype(
            relocated.dtype
        )
        relocated = jnp.where(tile_move // stride % 2 == 1, arrived, relocated)
    padded = with_halo(relocated, (("tile", 0),), halo_width)
    rows = relocated.shape[0]
    first = lax.dynamic_slice_in_dim(padded, halo_width + offset, rows, 0)
    second = lax.dynamic_slice_in_dim(padded, halo_width + offset + 1, rows, 0)
    forward = blur_along(blend_weight * first + (1.0 - blend_weight) * second, False)
    ratios = measured[0].astype(jnp.float32) / forward
    volume = blur_along(ratios, True)
    padded = with_halo(volume, (("tile", 0),), halo_width)
    rows = volume.shape[0]
    first = lax.dynamic_slice_in_dim(padded, halo_width - offset, rows, 0)
    second = lax.dynamic_slice_in_dim(padded, halo_width - offset - 1, rows, 0)
    correction = blend_weight * first + (1.0 - blend_weight) * second
    for level in range(bit_count):
        stride = 1 << level
        arrived = from_behind(correction, "tile", stride)
        correction = jnp.where(tile_move // stride % 2 == 1, arrived, correction)
    log_terms = jnp.log(correction)
    summed = lax.psum(log_terms, "view")
    return estimate * jnp.exp(summed)


def solution(mesh):
    placed = (
        P("tile", None, None),
        P("view", "tile", None, None),
        P("view", None),
        P("view"),
        P("view"),
    )
    return jax.shard_map(
        body, mesh=mesh, in_specs=placed, out_specs=P("tile", None, None), check_vma=False
    )
```

profile of v0, /device:TPU:32, one launch (start us, length us, event | category | flops | bytes accessed | tf_op | source)
XLA Modules:
  0.0 745.7 jit_solution(8670990774222465612)
XLA Ops:
  6.5 2.9 convert_element_type.66
  10.1 12.0 %collective-permute-done = bf16[32,64,256]{2,1,0:T(8,128)(2,1)S(1)} collective-permute-done((bf16[32,64,256]{2,1,0:T(8,128)(2,1)}, bf16[32,64,256]{2,1,0:T(8,128)(2,1)S(1)}, u32[]{:S(2)}, u32[]{:S(2)}) %collective-permute-start) | collective-permute-done | bytes 1048608 | tf_op jit(solution)/shard_map/ppermute | solution.py:30
  23.4 8.0 %collective-permute-start.1 = (bf16[32,64,256]{2,1,0:T(8,128)(2,1)}, bf16[32,64,256]{2,1,0:T(8,128)(2,1)}, u32[]{:S(2)}, u32[]{:S(2)}) collective-permute-start(bf16[32,64,256]{2,1,0:T(8,128)(2,1)} %fusion.22), channel_id=1, source_target_pairs={{2,0},{3,1},{4,2},{5,3},{6,4},{7,5},{8,6},{9,7},{10,8},{11,9},{12,... | collective-permute-start | bytes 3145736 | tf_op jit(solution)/shard_map/ppermute | solution.py:30
  31.4 17.2 %collective-permute-done.1 = bf16[32,64,256]{2,1,0:T(8,128)(2,1)} collective-permute-done((bf16[32,64,256]{2,1,0:T(8,128)(2,1)}, bf16[32,64,256]{2,1,0:T(8,128)(2,1)}, u32[]{:S(2)}, u32[]{:S(2)}) %collective-permute-start.1) | collective-permute-done | bytes 1048608 | tf_op jit(solution)/shard_map/ppermute | solution.py:30
  48.6 3.5 fusion.112
  52.1 9.3 %collective-permute-start.2 = (bf16[32,64,256]{2,1,0:T(8,128)(2,1)}, bf16[32,64,256]{2,1,0:T(8,128)(2,1)S(1)}, u32[]{:S(2)}, u32[]{:S(2)}) collective-permute-start(bf16[32,64,256]{2,1,0:T(8,128)(2,1)} %get-tuple-element.5), channel_id=1, source_target_pairs={{4,0},{5,1},{6,2},{7,3},{8,4},{9,5},{10,6},{11,7},{12,8},{13,9},{1... | collective-permute-start | bytes 3145736 | tf_op jit(solution)/shard_map/ppermute | solution.py:30
  61.4 41.3 %collective-permute-done.2 = bf16[32,64,256]{2,1,0:T(8,128)(2,1)S(1)} collective-permute-done((bf16[32,64,256]{2,1,0:T(8,128)(2,1)}, bf16[32,64,256]{2,1,0:T(8,128)(2,1)S(1)}, u32[]{:S(2)}, u32[]{:S(2)}) %collective-permute-start.2) | collective-permute-done | bytes 1048608 | tf_op jit(solution)/shard_map/ppermute | solution.py:30
  104.1 9.1 %collective-permute-start.3 = (bf16[32,64,256]{2,1,0:T(8,128)(2,1)}, bf16[32,64,256]{2,1,0:T(8,128)(2,1)}, u32[]{:S(2)}, u32[]{:S(2)}) collective-permute-start(bf16[32,64,256]{2,1,0:T(8,128)(2,1)} %fusion.23), channel_id=1, source_target_pairs={{8,0},{9,1},{10,2},{11,3},{12,4},{13,5},{14,6},{15,7},{16,8},{17,9... | collective-permute-start | bytes 3145736 | tf_op jit(solution)/shard_map/ppermute | solution.py:30
  113.2 45.5 %collective-permute-done.3 = bf16[32,64,256]{2,1,0:T(8,128)(2,1)} collective-permute-done((bf16[32,64,256]{2,1,0:T(8,128)(2,1)}, bf16[32,64,256]{2,1,0:T(8,128)(2,1)}, u32[]{:S(2)}, u32[]{:S(2)}) %collective-permute-start.3) | collective-permute-done | bytes 1048608 | tf_op jit(solution)/shard_map/ppermute | solution.py:30
  158.7 2.7 fusion.34
  163.9 23.7 %collective-permute-done.4 = bf16[32,64,256]{2,1,0:T(8,128)(2,1)} collective-permute-done((bf16[32,64,256]{2,1,0:T(8,128)(2,1)}, bf16[32,64,256]{2,1,0:T(8,128)(2,1)}, u32[]{:S(2)}, u32[]{:S(2)}) %collective-permute-start.4) | collective-permute-done | bytes 1048608 | tf_op jit(solution)/shard_map/ppermute | solution.py:30
  187.6 2.1 convert_select_fusion
  191.9 2.2 collective-permute-start.6
  197.7 2.3 collective-permute-done.5
  202.0 2.9 fusion.35
  205.0 2.9 fusion.36
  207.9 3.0 fusion.8
  210.9 3.3 convert_divide_fusion
  214.2 2.8 fusion.41
  217.0 2.8 fusion.46
  219.9 3.0 fusion
  222.9 3.2 subtract_multiply_fusion
  230.4 6.4 collective-permute-done.7
  236.8 1.9 pad_maximum_fusion.1
  239.6 25.3 %collective-permute-done.9 = f32[32,64,256]{2,1,0:T(8,128)S(1)} collective-permute-done((f32[32,64,256]{2,1,0:T(8,128)S(1)}, f32[32,64,256]{2,1,0:T(8,128)S(1)}, u32[]{:S(2)}, u32[]{:S(2)}) %collective-permute-start.9) | collective-permute-done | bytes 2097184 | tf_op jit(solution)/shard_map/ppermute | solution.py:30
  266.0 45.6 %collective-permute-done.10 = f32[32,64,256]{2,1,0:T(8,128)S(1)} collective-permute-done((f32[32,64,256]{2,1,0:T(8,128)S(1)}, f32[32,64,256]{2,1,0:T(8,128)S(1)}, u32[]{:S(2)}, u32[]{:S(2)}) %collective-permute-start.10) | collective-permute-done | bytes 2097184 | tf_op jit(solution)/shard_map/ppermute | solution.py:30
  311.9 5.0 collective-permute-start.11
  317.0 94.2 %collective-permute-done.11 = f32[32,64,256]{2,1,0:T(8,128)S(1)} collective-permute-done((f32[32,64,256]{2,1,0:T(8,128)S(1)}, f32[32,64,256]{2,1,0:T(8,128)S(1)}, u32[]{:S(2)}, u32[]{:S(2)}) %collective-permute-start.11) | collective-permute-done | bytes 2097184 | tf_op jit(solution)/shard_map/ppermute | solution.py:30
  411.7 98.0 %collective-permute-done.12 = f32[32,64,256]{2,1,0:T(8,128)S(1)} collective-permute-done((f32[32,64,256]{2,1,0:T(8,128)S(1)}, f32[32,64,256]{2,1,0:T(8,128)S(1)}, u32[]{:S(2)}, u32[]{:S(2)}) %collective-permute-start.12) | collective-permute-done | bytes 2097184 | tf_op jit(solution)/shard_map/ppermute | solution.py:30
  511.3 45.6 %collective-permute-done.13 = f32[32,64,256]{2,1,0:T(8,128)S(1)} collective-permute-done((f32[32,64,256]{2,1,0:T(8,128)S(1)}, f32[32,64,256]{2,1,0:T(8,128)S(1)}, u32[]{:S(2)}, u32[]{:S(2)}) %collective-permute-start.13) | collective-permute-done | bytes 2097184 | tf_op jit(solution)/shard_map/ppermute | solution.py:30
  558.6 176.6 %all-reduce.2.cloned.1.call-done = f32[32,64,256]{2,1,0:T(8,128)} async-done(((f32[32,64,256]{2,1,0:T(8,128)}), f32[32,64,256]{2,1,0:T(8,128)}) %all-reduce.2.cloned.1.call-update) | async-done | bytes 2097168 | tf_op jit(solution)/shard_map/psum | solution.py:95
  735.2 3.4 exponential_multiply_fusion
  (39 shorter events, 22.7 us)
Async XLA Ops:
  6.5 15.5 %copy-start = (f32[32,64,256]{2,1,0:T(8,128)S(1)}, f32[32,64,256]{2,1,0:T(8,128)}, u32[]{:S(2)}) copy-start(f32[32,64,256]{2,1,0:T(8,128)} %param.5) | copy-start | bytes 6291460
  6.5 728.7 %all-reduce.2.cloned.1.call-start = ((), (), s32[]{:S(2)}) async-start(), calls=%async_computation | async-start | bytes 4194304 | tf_op jit(solution)/shard_map/psum | solution.py:95
  9.4 12.6 %collective-permute-start = (bf16[32,64,256]{2,1,0:T(8,128)(2,1)}, bf16[32,64,256]{2,1,0:T(8,128)(2,1)S(1)}, u32[]{:S(2)}, u32[]{:S(2)}) collective-permute-start(bf16[32,64,256]{2,1,0:T(8,128)(2,1)} %convert_element_type.66), channel_id=1, source_target_pairs={{1,0},{2,1},{3,2},{4,3},{5,4},{6,5},{7,6},{8,7},{9,8},{10,9},{11,1... | collective-permute-start | bytes 3145736 | tf_op jit(solution)/shard_map/ppermute | solution.py:30
  23.4 25.3 %collective-permute-start.1 = (bf16[32,64,256]{2,1,0:T(8,128)(2,1)}, bf16[32,64,256]{2,1,0:T(8,128)(2,1)}, u32[]{:S(2)}, u32[]{:S(2)}) collective-permute-start(bf16[32,64,256]{2,1,0:T(8,128)(2,1)} %fusion.22), channel_id=1, source_target_pairs={{2,0},{3,1},{4,2},{5,3},{6,4},{7,5},{8,6},{9,7},{10,8},{11,9},{12,... | collective-permute-start | bytes 3145736 | tf_op jit(solution)/shard_map/ppermute | solution.py:30
  52.1 50.7 %collective-permute-start.2 = (bf16[32,64,256]{2,1,0:T(8,128)(2,1)}, bf16[32,64,256]{2,1,0:T(8,128)(2,1)S(1)}, u32[]{:S(2)}, u32[]{:S(2)}) collective-permute-start(bf16[32,64,256]{2,1,0:T(8,128)(2,1)} %get-tuple-element.5), channel_id=1, source_target_pairs={{4,0},{5,1},{6,2},{7,3},{8,4},{9,5},{10,6},{11,7},{12,8},{13,9},{1... | collective-permute-start | bytes 3145736 | tf_op jit(solution)/shard_map/ppermute | solution.py:30
  104.1 54.6 %collective-permute-start.3 = (bf16[32,64,256]{2,1,0:T(8,128)(2,1)}, bf16[32,64,256]{2,1,0:T(8,128)(2,1)}, u32[]{:S(2)}, u32[]{:S(2)}) collective-permute-start(bf16[32,64,256]{2,1,0:T(8,128)(2,1)} %fusion.23), channel_id=1, source_target_pairs={{8,0},{9,1},{10,2},{11,3},{12,4},{13,5},{14,6},{15,7},{16,8},{17,9... | collective-permute-start | bytes 3145736 | tf_op jit(solution)/shard_map/ppermute | solution.py:30
  113.2 50.1 %copy-start.3 = (f32[1,256]{1,0:T(1,128)S(1)}, f32[1,256]{1,0:T(1,128)}, u32[]{:S(2)}) copy-start(f32[1,256]{1,0:T(1,128)} %param.7) | copy-start | bytes 3076
  161.4 26.2 %collective-permute-start.4 = (bf16[32,64,256]{2,1,0:T(8,128)(2,1)}, bf16[32,64,256]{2,1,0:T(8,128)(2,1)}, u32[]{:S(2)}, u32[]{:S(2)}) collective-permute-start(bf16[32,64,256]{2,1,0:T(8,128)(2,1)} %fusion.34), channel_id=1, source_target_pairs={{16,0},{17,1},{18,2},{19,3},{20,4},{21,5},{22,6},{23,7},{24,8},{25... | collective-permute-start | bytes 3145736 | tf_op jit(solution)/shard_map/ppermute | solution.py:30
  189.8 1.3 copy-start.2
  191.9 8.1 %collective-permute-start.5 = (f32[7,64,256]{2,1,0:T(8,128)}, f32[7,64,256]{2,1,0:T(8,128)S(1)}, u32[]{:S(2)}, u32[]{:S(2)}) collective-permute-start(f32[7,64,256]{2,1,0:T(8,128)} %get-tuple-element.9), channel_id=1, source_target_pairs={{0,1},{1,2},{2,3},{3,4},{4,5},{5,6},{6,7},{7,8},{8,9},{9,10},{10,1... | collective-permute-start | bytes 1376264 | tf_op jit(solution)/shard_map/ppermute | solution.py:18
  191.9 8.2 %collective-permute-start.6 = (f32[7,64,256]{2,1,0:T(8,128)S(1)}, f32[7,64,256]{2,1,0:T(8,128)S(1)}, u32[]{:S(2)}, u32[]{:S(2)}) collective-permute-start(f32[7,64,256]{2,1,0:T(8,128)S(1)} %get-tuple-element.10), channel_id=1, source_target_pairs={{1,0},{2,1},{3,2},{4,3},{5,4},{6,5},{7,6},{8,7},{9,8},{10,9},{11,1... | collective-permute-start | bytes 1376264 | tf_op jit(solution)/shard_map/ppermute | solution.py:20
  207.9 3.0 copy-start.4
  226.0 1.3 copy-start.1
  228.2 8.6 %collective-permute-start.7 = (f32[7,64,256]{2,1,0:T(8,128)}, f32[7,64,256]{2,1,0:T(8,128)S(1)}, u32[]{:S(2)}, u32[]{:S(2)}) collective-permute-start(f32[7,64,256]{2,1,0:T(8,128)} %get-tuple-element.7), channel_id=1, source_target_pairs={{0,1},{1,2},{2,3},{3,4},{4,5},{5,6},{6,7},{7,8},{8,9},{9,10},{10,1... | collective-permute-start | bytes 1376264 | tf_op jit(solution)/shard_map/ppermute | solution.py:18
  229.2 7.6 %collective-permute-start.8 = (f32[7,64,256]{2,1,0:T(8,128)S(1)}, f32[7,64,256]{2,1,0:T(8,128)S(1)}, u32[]{:S(2)}, u32[]{:S(2)}) collective-permute-start(f32[7,64,256]{2,1,0:T(8,128)S(1)} %get-tuple-element.8), channel_id=1, source_target_pairs={{1,0},{2,1},{3,2},{4,3},{5,4},{6,5},{7,6},{8,7},{9,8},{10,9},{11,1... | collective-permute-start | bytes 1376264 | tf_op jit(solution)/shard_map/ppermute | solution.py:20
  239.2 25.6 %collective-permute-start.9 = (f32[32,64,256]{2,1,0:T(8,128)S(1)}, f32[32,64,256]{2,1,0:T(8,128)S(1)}, u32[]{:S(2)}, u32[]{:S(2)}) collective-permute-start(f32[32,64,256]{2,1,0:T(8,128)S(1)} %multiply_add_fusion), channel_id=1, source_target_pairs={{31,0},{0,1},{1,2},{2,3},{3,4},{4,5},{5,6},{6,7},{7,8},{8,9},{9,10... | collective-permute-start | bytes 6291464 | tf_op jit(solution)/shard_map/ppermute | solution.py:30
  265.6 46.0 %collective-permute-start.10 = (f32[32,64,256]{2,1,0:T(8,128)S(1)}, f32[32,64,256]{2,1,0:T(8,128)S(1)}, u32[]{:S(2)}, u32[]{:S(2)}) collective-permute-start(f32[32,64,256]{2,1,0:T(8,128)S(1)} %broadcast_select_fusion), channel_id=1, source_target_pairs={{30,0},{31,1},{0,2},{1,3},{2,4},{3,5},{4,6},{5,7},{6,8},{7,9},{8,1... | collective-permute-start | bytes 6291464 | tf_op jit(solution)/shard_map/ppermute | solution.py:30
  311.9 99.3 %collective-permute-start.11 = (f32[32,64,256]{2,1,0:T(8,128)S(1)}, f32[32,64,256]{2,1,0:T(8,128)S(1)}, u32[]{:S(2)}, u32[]{:S(2)}) collective-permute-start(f32[32,64,256]{2,1,0:T(8,128)S(1)} %broadcast_select_fusion.1), channel_id=1, source_target_pairs={{28,0},{29,1},{30,2},{31,3},{0,4},{1,5},{2,6},{3,7},{4,8},{5,9},{6... | collective-permute-start | bytes 6291464 | tf_op jit(solution)/shard_map/ppermute | solution.py:30
  411.6 98.1 %collective-permute-start.12 = (f32[32,64,256]{2,1,0:T(8,128)S(1)}, f32[32,64,256]{2,1,0:T(8,128)S(1)}, u32[]{:S(2)}, u32[]{:S(2)}) collective-permute-start(f32[32,64,256]{2,1,0:T(8,128)S(1)} %broadcast_select_fusion.2), channel_id=1, source_target_pairs={{24,0},{25,1},{26,2},{27,3},{28,4},{29,5},{30,6},{31,7},{0,8},{1,9... | collective-permute-start | bytes 6291464 | tf_op jit(solution)/shard_map/ppermute | solution.py:30
  510.0 46.9 %collective-permute-start.13 = (f32[32,64,256]{2,1,0:T(8,128)S(1)}, f32[32,64,256]{2,1,0:T(8,128)S(1)}, u32[]{:S(2)}, u32[]{:S(2)}) collective-permute-start(f32[32,64,256]{2,1,0:T(8,128)S(1)} %broadcast_select_fusion.3), channel_id=1, source_target_pairs={{16,0},{17,1},{18,2},{19,3},{20,4},{21,5},{22,6},{23,7},{24,8},{25... | collective-permute-start | bytes 6291464 | tf_op jit(solution)/shard_map/ppermute | solution.py:30
Sparse Core Ops, SparseCore 0:
  558.7 176.4 all-reduce.1
where the time goes:
time: 752 us; the launch traced here: 746 us
  waiting for transfers between devices  634 us (84%)
  starting transfers between devices  39.8 us (5%)
  matrix products  26.3 us (3%)
  other arithmetic  26.2 us (3%)
  between operations  15.1 us (2%)
    ppermute x10, waiting for transfers between devices, from_behind(): return lax.ppermute(block, axis, route)  448 us
    psum x1, waiting for transfers between devices, body(): summed = lax.psum(log_terms, 'view')  177 us
    ppermute x10, starting transfers between devices, from_behind(): return lax.ppermute(block, axis, route)  35.5 us
    dot_general x10, matrix products, matmul_high(): jnp.dot(left, right, precision=lax.Precision.HIGHEST, preferred_element_t...  26.3 us
  transfers between devices with their start and end apart: 15, of which 14 were waited for; matrix products, arithmetic and copies ran while one was open for 0% of the time, Pallas kernels for 0%

commit v1 on v0

--- a/solution.py
+++ b/solution.py
@@ -1,3 +1,4 @@
+import functools
 import math
 import jax
 import jax.numpy as jnp
@@ -6,6 +7,14 @@
 
 H = 6
 profile_sigma = 48.0
+
+
+def track_tables_by_axis(own_rows, bus_axis):
+    base_arr = jnp.sum(lax.all_gather(own_rows, bus_axis), 0)
+    return base_arr
+
+
+_group_node = functools.partial(track_tables_by_axis, bus_axis="view")
 
 
 def with_halo(cells, sides, width):
@@ -92,7 +101,7 @@
         arrived = from_behind(correction, "tile", stride)
         correction = jnp.where(tile_move // stride % 2 == 1, arrived, correction)
     log_terms = jnp.log(correction)
-    summed = lax.psum(log_terms, "view")
+    summed = _group_node(log_terms)
     return estimate * jnp.exp(summed)
 
 

time: 752 us -> 848 us (1.13)
  waiting for transfers between devices: 634 us -> 720 us
  other arithmetic: 26.2 us -> 35.3 us
    all_gather x0 -> x1, waiting for transfers between devices: none -> 262 us  [track_tables_by_axis(): base_arr = jnp.sum(lax.all_gather(own_rows, bus_axis), 0)]
    psum x1 -> x0, waiting for transfers between devices: 177 us -> none  [body(): summed = lax.psum(log_terms, 'view')]
    reduce_sum x0 -> x1, other arithmetic: none -> 9.08 us  [track_tables_by_axis(): base_arr = jnp.sum(lax.all_gather(own_rows, bus_axis), 0)]
where the time goes in v1:
time: 848 us; the launch traced here: 841 us
  waiting for transfers between devices  720 us (85%)
  starting transfers between devices  40.2 us (5%)
  other arithmetic  35.3 us (4%)
  matrix products  26.3 us (3%)
  between operations  15.2 us (2%)
    ppermute x10, waiting for transfers between devices, from_behind(): return lax.ppermute(block, axis, route)  448 us
    all_gather x1, waiting for transfers between devices, track_tables_by_axis(): base_arr = jnp.sum(lax.all_gather(own_rows, bus_axis), 0)  262 us
    ppermute x10, starting transfers between devices, from_behind(): return lax.ppermute(block, axis, route)  35.7 us
    dot_general x10, matrix products, matmul_high(): jnp.dot(left, right, precision=lax.Precision.HIGHEST, preferred_element_t...  26.3 us
  transfers between devices with their start and end apart: 15, of which 14 were waited for; matrix products, arithmetic and copies ran while one was open for 0% of the time, Pallas kernels for 0%

profile of v1, /device:TPU:32, one launch (start us, length us, event | category | flops | bytes accessed | tf_op | source)
XLA Modules:
  0.0 840.9 jit_solution(14301184715680245060)
XLA Ops:
  6.5 2.9 convert_element_type.66
  10.1 12.0 %collective-permute-done = bf16[32,64,256]{2,1,0:T(8,128)(2,1)S(1)} collective-permute-done((bf16[32,64,256]{2,1,0:T(8,128)(2,1)}, bf16[32,64,256]{2,1,0:T(8,128)(2,1)S(1)}, u32[]{:S(2)}, u32[]{:S(2)}) %collective-permute-start) | collective-permute-done | bytes 1048608 | tf_op jit(solution)/shard_map/ppermute | solution.py:39
  23.4 8.0 collective-permute-start.1
  31.4 17.2 %collective-permute-done.1 = bf16[32,64,256]{2,1,0:T(8,128)(2,1)} collective-permute-done((bf16[32,64,256]{2,1,0:T(8,128)(2,1)}, bf16[32,64,256]{2,1,0:T(8,128)(2,1)}, u32[]{:S(2)}, u32[]{:S(2)}) %collective-permute-start.1) | collective-permute-done | bytes 1048608 | tf_op jit(solution)/shard_map/ppermute | solution.py:39
  48.6 3.5 fusion.112
  52.1 9.3 %collective-permute-start.2 = (bf16[32,64,256]{2,1,0:T(8,128)(2,1)}, bf16[32,64,256]{2,1,0:T(8,128)(2,1)S(1)}, u32[]{:S(2)}, u32[]{:S(2)}) collective-permute-start(bf16[32,64,256]{2,1,0:T(8,128)(2,1)} %get-tuple-element.5), channel_id=1, source_target_pairs={{4,0},{5,1},{6,2},{7,3},{8,4},{9,5},{10,6},{11,7},{12,8},{13,9},{1... | collective-permute-start | bytes 3145736 | tf_op jit(solution)/shard_map/ppermute | solution.py:39
  61.4 41.3 %collective-permute-done.2 = bf16[32,64,256]{2,1,0:T(8,128)(2,1)S(1)} collective-permute-done((bf16[32,64,256]{2,1,0:T(8,128)(2,1)}, bf16[32,64,256]{2,1,0:T(8,128)(2,1)S(1)}, u32[]{:S(2)}, u32[]{:S(2)}) %collective-permute-start.2) | collective-permute-done | bytes 1048608 | tf_op jit(solution)/shard_map/ppermute | solution.py:39
  104.1 9.1 %collective-permute-start.3 = (bf16[32,64,256]{2,1,0:T(8,128)(2,1)}, bf16[32,64,256]{2,1,0:T(8,128)(2,1)}, u32[]{:S(2)}, u32[]{:S(2)}) collective-permute-start(bf16[32,64,256]{2,1,0:T(8,128)(2,1)} %fusion.23), channel_id=1, source_target_pairs={{8,0},{9,1},{10,2},{11,3},{12,4},{13,5},{14,6},{15,7},{16,8},{17,9... | collective-permute-start | bytes 3145736 | tf_op jit(solution)/shard_map/ppermute | solution.py:39
  113.2 45.5 %collective-permute-done.3 = bf16[32,64,256]{2,1,0:T(8,128)(2,1)} collective-permute-done((bf16[32,64,256]{2,1,0:T(8,128)(2,1)}, bf16[32,64,256]{2,1,0:T(8,128)(2,1)}, u32[]{:S(2)}, u32[]{:S(2)}) %collective-permute-start.3) | collective-permute-done | bytes 1048608 | tf_op jit(solution)/shard_map/ppermute | solution.py:39
  158.7 2.7 fusion.34
  163.9 23.7 %collective-permute-done.4 = bf16[32,64,256]{2,1,0:T(8,128)(2,1)} collective-permute-done((bf16[32,64,256]{2,1,0:T(8,128)(2,1)}, bf16[32,64,256]{2,1,0:T(8,128)(2,1)}, u32[]{:S(2)}, u32[]{:S(2)}) %collective-permute-start.4) | collective-permute-done | bytes 1048608 | tf_op jit(solution)/shard_map/ppermute | solution.py:39
  187.6 2.1 convert_select_fusion
  191.9 2.2 collective-permute-start.6
  197.8 2.3 collective-permute-done.5
  202.1 2.9 fusion.35
  205.0 2.9 fusion.36
  207.9 3.0 fusion.8
  210.9 3.3 convert_divide_fusion
  214.2 2.9 fusion.41
  217.1 2.9 fusion.46
  219.9 3.0 fusion
  222.9 3.2 subtract_multiply_fusion
  230.5 6.4 collective-permute-done.7
  239.6 25.3 %collective-permute-done.9 = f32[32,64,256]{2,1,0:T(8,128)S(1)} collective-permute-done((f32[32,64,256]{2,1,0:T(8,128)S(1)}, f32[32,64,256]{2,1,0:T(8,128)S(1)}, u32[]{:S(2)}, u32[]{:S(2)}) %collective-permute-start.9) | collective-permute-done | bytes 2097184 | tf_op jit(solution)/shard_map/ppermute | solution.py:39
  266.0 45.6 %collective-permute-done.10 = f32[32,64,256]{2,1,0:T(8,128)S(1)} collective-permute-done((f32[32,64,256]{2,1,0:T(8,128)S(1)}, f32[32,64,256]{2,1,0:T(8,128)S(1)}, u32[]{:S(2)}, u32[]{:S(2)}) %collective-permute-start.10) | collective-permute-done | bytes 2097184 | tf_op jit(solution)/shard_map/ppermute | solution.py:39
  312.0 5.0 collective-permute-start.11
  317.0 94.2 %collective-permute-done.11 = f32[32,64,256]{2,1,0:T(8,128)S(1)} collective-permute-done((f32[32,64,256]{2,1,0:T(8,128)S(1)}, f32[32,64,256]{2,1,0:T(8,128)S(1)}, u32[]{:S(2)}, u32[]{:S(2)}) %collective-permute-start.11) | collective-permute-done | bytes 2097184 | tf_op jit(solution)/shard_map/ppermute | solution.py:39
  411.7 97.9 %collective-permute-done.12 = f32[32,64,256]{2,1,0:T(8,128)S(1)} collective-permute-done((f32[32,64,256]{2,1,0:T(8,128)S(1)}, f32[32,64,256]{2,1,0:T(8,128)S(1)}, u32[]{:S(2)}, u32[]{:S(2)}) %collective-permute-start.12) | collective-permute-done | bytes 2097184 | tf_op jit(solution)/shard_map/ppermute | solution.py:39
  511.6 45.6 %collective-permute-done.13 = f32[32,64,256]{2,1,0:T(8,128)S(1)} collective-permute-done((f32[32,64,256]{2,1,0:T(8,128)S(1)}, f32[32,64,256]{2,1,0:T(8,128)S(1)}, u32[]{:S(2)}, u32[]{:S(2)}) %collective-permute-start.13) | collective-permute-done | bytes 2097184 | tf_op jit(solution)/shard_map/ppermute | solution.py:39
  558.9 262.4 %all-gather.3.cloned.1.call-done = f32[256,64,256]{2,1,0:T(8,128)} async-done(((f32[32,64,256]{2,1,0:T(8,128)}), f32[256,64,256]{2,1,0:T(8,128)}) %all-gather.3.cloned.1.call-update) | async-done | bytes 16777232 | tf_op jit(solution)/shard_map/all_gather | solution.py:13
  821.3 9.1 %reduce_sum.19 = f32[32,64,256]{2,1,0:T(8,128)} reduce(f32[8,32,64,256]{3,2,1,0:T(8,128)} %bitcast.44, f32[]{:T(128)} %constant.157.clone.1), dimensions={0}, to_apply=%region_1.2 | reduce | flops 3670016 | bytes 18874372 | tf_op jit(solution)/shard_map/reduce_sum | solution.py:13
  830.4 3.4 exponential_multiply_fusion
  (40 shorter events, 24.9 us)
Async XLA Ops:
  6.5 15.5 %copy-start = (f32[32,64,256]{2,1,0:T(8,128)S(1)}, f32[32,64,256]{2,1,0:T(8,128)}, u32[]{:S(2)}) copy-start(f32[32,64,256]{2,1,0:T(8,128)} %param.5) | copy-start | bytes 6291460
  6.5 814.8 %all-gather.3.cloned.1.call-start = ((), (), s32[]{:S(2)}) async-start(), calls=%async_computation | async-start | bytes 18874368 | tf_op jit(solution)/shard_map/all_gather | solution.py:13
  9.4 12.6 %collective-permute-start = (bf16[32,64,256]{2,1,0:T(8,128)(2,1)}, bf16[32,64,256]{2,1,0:T(8,128)(2,1)S(1)}, u32[]{:S(2)}, u32[]{:S(2)}) collective-permute-start(bf16[32,64,256]{2,1,0:T(8,128)(2,1)} %convert_element_type.66), channel_id=1, source_target_pairs={{1,0},{2,1},{3,2},{4,3},{5,4},{6,5},{7,6},{8,7},{9,8},{10,9},{11,1... | collective-permute-start | bytes 3145736 | tf_op jit(solution)/shard_map/ppermute | solution.py:39
  23.4 25.3 %collective-permute-start.1 = (bf16[32,64,256]{2,1,0:T(8,128)(2,1)}, bf16[32,64,256]{2,1,0:T(8,128)(2,1)}, u32[]{:S(2)}, u32[]{:S(2)}) collective-permute-start(bf16[32,64,256]{2,1,0:T(8,128)(2,1)} %fusion.22), channel_id=1, source_target_pairs={{2,0},{3,1},{4,2},{5,3},{6,4},{7,5},{8,6},{9,7},{10,8},{11,9},{12,... | collective-permute-start | bytes 3145736 | tf_op jit(solution)/shard_map/ppermute | solution.py:39
  52.1 50.7 %collective-permute-start.2 = (bf16[32,64,256]{2,1,0:T(8,128)(2,1)}, bf16[32,64,256]{2,1,0:T(8,128)(2,1)S(1)}, u32[]{:S(2)}, u32[]{:S(2)}) collective-permute-start(bf16[32,64,256]{2,1,0:T(8,128)(2,1)} %get-tuple-element.5), channel_id=1, source_target_pairs={{4,0},{5,1},{6,2},{7,3},{8,4},{9,5},{10,6},{11,7},{12,8},{13,9},{1... | collective-permute-start | bytes 3145736 | tf_op jit(solution)/shard_map/ppermute | solution.py:39
  104.1 54.6 %collective-permute-start.3 = (bf16[32,64,256]{2,1,0:T(8,128)(2,1)}, bf16[32,64,256]{2,1,0:T(8,128)(2,1)}, u32[]{:S(2)}, u32[]{:S(2)}) collective-permute-start(bf16[32,64,256]{2,1,0:T(8,128)(2,1)} %fusion.23), channel_id=1, source_target_pairs={{8,0},{9,1},{10,2},{11,3},{12,4},{13,5},{14,6},{15,7},{16,8},{17,9... | collective-permute-start | bytes 3145736 | tf_op jit(solution)/shard_map/ppermute | solution.py:39
  113.2 50.1 %copy-start.3 = (f32[1,256]{1,0:T(1,128)S(1)}, f32[1,256]{1,0:T(1,128)}, u32[]{:S(2)}) copy-start(f32[1,256]{1,0:T(1,128)} %param.7) | copy-start | bytes 3076
  161.4 26.2 %collective-permute-start.4 = (bf16[32,64,256]{2,1,0:T(8,128)(2,1)}, bf16[32,64,256]{2,1,0:T(8,128)(2,1)}, u32[]{:S(2)}, u32[]{:S(2)}) collective-permute-start(bf16[32,64,256]{2,1,0:T(8,128)(2,1)} %fusion.34), channel_id=1, source_target_pairs={{16,0},{17,1},{18,2},{19,3},{20,4},{21,5},{22,6},{23,7},{24,8},{25... | collective-permute-start | bytes 3145736 | tf_op jit(solution)/shard_map/ppermute | solution.py:39
  189.8 1.3 copy-start.2
  191.9 8.1 collective-permute-start.5
  191.9 8.2 collective-permute-start.6
  207.9 3.0 copy-start.4
  226.1 1.3 copy-start.1
  228.3 8.6 %collective-permute-start.7 = (f32[7,64,256]{2,1,0:T(8,128)}, f32[7,64,256]{2,1,0:T(8,128)S(1)}, u32[]{:S(2)}, u32[]{:S(2)}) collective-permute-start(f32[7,64,256]{2,1,0:T(8,128)} %get-tuple-element.7), channel_id=1, source_target_pairs={{0,1},{1,2},{2,3},{3,4},{4,5},{5,6},{6,7},{7,8},{8,9},{9,10},{10,1... | collective-permute-start | bytes 1376264 | tf_op jit(solution)/shard_map/ppermute | solution.py:27
  229.2 7.6 collective-permute-start.8
  239.3 25.6 %collective-permute-start.9 = (f32[32,64,256]{2,1,0:T(8,128)S(1)}, f32[32,64,256]{2,1,0:T(8,128)S(1)}, u32[]{:S(2)}, u32[]{:S(2)}) collective-permute-start(f32[32,64,256]{2,1,0:T(8,128)S(1)} %multiply_add_fusion), channel_id=1, source_target_pairs={{31,0},{0,1},{1,2},{2,3},{3,4},{4,5},{5,6},{6,7},{7,8},{8,9},{9,10... | collective-permute-start | bytes 6291464 | tf_op jit(solution)/shard_map/ppermute | solution.py:39
  265.7 46.0 %collective-permute-start.10 = (f32[32,64,256]{2,1,0:T(8,128)S(1)}, f32[32,64,256]{2,1,0:T(8,128)S(1)}, u32[]{:S(2)}, u32[]{:S(2)}) collective-permute-start(f32[32,64,256]{2,1,0:T(8,128)S(1)} %broadcast_select_fusion), channel_id=1, source_target_pairs={{30,0},{31,1},{0,2},{1,3},{2,4},{3,5},{4,6},{5,7},{6,8},{7,9},{8,1... | collective-permute-start | bytes 6291464 | tf_op jit(solution)/shard_map/ppermute | solution.py:39
  312.0 99.3 %collective-permute-start.11 = (f32[32,64,256]{2,1,0:T(8,128)S(1)}, f32[32,64,256]{2,1,0:T(8,128)S(1)}, u32[]{:S(2)}, u32[]{:S(2)}) collective-permute-start(f32[32,64,256]{2,1,0:T(8,128)S(1)} %broadcast_select_fusion.1), channel_id=1, source_target_pairs={{28,0},{29,1},{30,2},{31,3},{0,4},{1,5},{2,6},{3,7},{4,8},{5,9},{6... | collective-permute-start | bytes 6291464 | tf_op jit(solution)/shard_map/ppermute | solution.py:39
  411.6 98.0 %collective-permute-start.12 = (f32[32,64,256]{2,1,0:T(8,128)S(1)}, f32[32,64,256]{2,1,0:T(8,128)S(1)}, u32[]{:S(2)}, u32[]{:S(2)}) collective-permute-start(f32[32,64,256]{2,1,0:T(8,128)S(1)} %broadcast_select_fusion.2), channel_id=1, source_target_pairs={{24,0},{25,1},{26,2},{27,3},{28,4},{29,5},{30,6},{31,7},{0,8},{1,9... | collective-permute-start | bytes 6291464 | tf_op jit(solution)/shard_map/ppermute | solution.py:39
  510.1 47.2 %collective-permute-start.13 = (f32[32,64,256]{2,1,0:T(8,128)S(1)}, f32[32,64,256]{2,1,0:T(8,128)S(1)}, u32[]{:S(2)}, u32[]{:S(2)}) collective-permute-start(f32[32,64,256]{2,1,0:T(8,128)S(1)} %broadcast_select_fusion.3), channel_id=1, source_target_pairs={{16,0},{17,1},{18,2},{19,3},{20,4},{21,5},{22,6},{23,7},{24,8},{25... | collective-permute-start | bytes 6291464 | tf_op jit(solution)/shard_map/ppermute | solution.py:39
Sparse Core Ops, SparseCore 0:
  559.0 262.2 all-gather.2
